TPU v7x, 1024 devices: a whole 8x8x8 slice. The times are simulated.
1024 devices in a mesh: row: 32 (over y, x_hi, core), col: 32 (over z, x_lo).
Axes of the slice: x: 8 (x_hi: 2, x_lo: 4; x = x_hi * 4 + x_lo), y: 8, z: 8, core: 2. Of those that a mesh axis runs over, the one named last changes fastest.
Arguments:
- tokens: bfloat16 [512, 8192], P('col', 'row'), may hold values from -6 to 6
- w_packed: bfloat16 [32, 32, 14, 128, 128], P('row', 'col'), may hold values from -0.09375 to 0.09375
- kept_rows: int32 [32, 32, 14], P('row', 'col'), may hold values from 0 to 1, as said below
- kept_cols: int32 [32, 32, 14], P('row', 'col'), may hold values from 0 to 6, as said below
- kept_count: int32 [32, 32], P('row', 'col'), may hold values from 1 to 14, as said below
- grad_act: bfloat16 [512, 28672], P('row', 'col'), may hold values from -6 to 6
Outputs:
- activation: bfloat16 [512, 28672], P('row', 'col')
- input_grad: bfloat16 [512, 8192], P('col', 'row')
- weight_grad: bfloat16 [32, 32, 14, 128, 128], P('row', 'col')
Inputs may be any that keep to these rules, and one draw needn't show every extreme that they name: Within each tile, the 14 slots name every block of the tile once (kept_rows[r, c, s] * 7 + kept_cols[r, c, s] runs over all block places). `kept_cols`: see kept_rows. `kept_count`: some tile in every draw keeps all 14 blocks.
All inputs are finite; a program needn't handle non-finite values.
Results may differ from a plain program's by a relative error of at most 0.0049.
Values may be sent and summed in bfloat16 or wider, within the bound.
A program may use at most 32 MiB of HBM per device.

v0:
```python
import jax
import jax.numpy as jnp
from jax import lax
from jax.sharding import PartitionSpec as P

gelu_scale = 0.7978845608
gelu_cubic = 0.044715


def gelu_pair(hidden, cotangent):
    inner = gelu_scale * (hidden + gelu_cubic * hidden * hidden * hidden)
    tangent = jnp.tanh(inner)
    activation = (0.5 * hidden * (1.0 + tangent)).astype(jnp.bfloat16)
    slope = 0.5 * (1.0 + tangent) + 0.5 * hidden * (1.0 - tangent * tangent) * gelu_scale * (
        1.0 + 3.0 * gelu_cubic * hidden * hidden
    )
    slope_grad = (cotangent.astype(jnp.float32) * slope).astype(jnp.bfloat16)
    return (activation, slope_grad)


def on_device(tokens, w_packed, kept_rows, kept_cols, kept_count, grad_act):
    block_size = w_packed.shape[-1]
    slot_count = w_packed.shape[2]
    width_here = tokens.shape[1]
    hidden_here = grad_act.shape[1]
    row_blocks = width_here // block_size
    col_blocks = hidden_here // block_size
    live_slots = jnp.arange(slot_count) < kept_count[0, 0]
    row_pick = (
        (kept_rows[0, 0][:, None] == jnp.arange(row_blocks)[None, :]) & live_slots[:, None]
    ).astype(jnp.bfloat16)
    col_pick = (
        (kept_cols[0, 0][:, None] == jnp.arange(col_blocks)[None, :]) & live_slots[:, None]
    ).astype(jnp.bfloat16)
    weight_blocks = w_packed[0, 0]
    gathered = lax.all_gather(tokens, "col", axis=0, tiled=True)

    def pick_rows(features, rows_here):
        shaped = features.reshape(rows_here, row_blocks, block_size)
        return jnp.einsum(
            "nrk,sr->nsk", shaped, row_pick, preferred_element_type=jnp.float32
        ).astype(jnp.bfloat16)

    def pick_cols(hidden_rows, rows_here):
        shaped = hidden_rows.reshape(rows_here, col_blocks, block_size)
        return jnp.einsum(
            "ncj,sc->nsj", shaped, col_pick, preferred_element_type=jnp.float32
        ).astype(jnp.bfloat16)

    rows_here = grad_act.shape[0] * lax.axis_size("row")
    features = gathered
    product = jnp.einsum(
        "nsk,skj->nsj",
        pick_rows(features, rows_here),
        weight_blocks,
        preferred_element_type=jnp.float32,
    )
    placed = jnp.einsum(
        "nsj,sc->ncj", product, col_pick.astype(jnp.float32), precision=lax.Precision.HIGHEST
    )
    hidden = lax.psum_scatter(
        placed.reshape(rows_here, hidden_here), "row", scatter_dimension=0, tiled=True
    )
    activation, slope_grad = gelu_pair(hidden, grad_act)
    grad_all = lax.all_gather(slope_grad, "row", axis=0, tiled=True)
    rows_here = grad_all.shape[0]
    weight_sum = jnp.einsum(
        "nsi,nsj->sij",
        pick_rows(gathered, rows_here),
        pick_cols(grad_all, rows_here),
        preferred_element_type=jnp.float32,
    )
    rows_here = grad_all.shape[0]
    product = jnp.einsum(
        "nsj,sij->nsi",
        pick_cols(grad_all, rows_here),
        weight_blocks,
        preferred_element_type=jnp.float32,
    )
    placed = jnp.einsum(
        "nsi,sr->nri", product, row_pick.astype(jnp.float32), precision=lax.Precision.HIGHEST
    )
    input_grad = lax.psum_scatter(
        placed.reshape(rows_here, width_here), "col", scatter_dimension=0, tiled=True
    ).astype(jnp.bfloat16)
    weight_grad = weight_sum.astype(jnp.bfloat16)[None, None]
    return (activation, input_grad, weight_grad)


def solution(mesh):
    placed = (
        P("col", "row"),
        P("row", "col", None, None, None),
        P("row", "col", None),
        P("row", "col", None),
        P("row", "col"),
        P("row", "col"),
    )
    return jax.shard_map(
        on_device,
        mesh=mesh,
        in_specs=placed,
        out_specs=(P("row", "col"), P("col", "row"), P("row", "col", None, None, None)),
        check_vma=False,
    )
```

profile of v0, /device:TPU:16, one launch (start us, length us, event | category | flops | bytes accessed | tf_op | source)
XLA Modules:
  0.0 490.8 jit_solution(15187841866081611762)
XLA Ops:
  7.2 0.0 copy-start
  7.2 0.0 reduce-scatter.7.cloned.1.call-start
  7.9 93.3 %all_gather.6 = bf16[512,256]{1,0:T(8,128)(2,1)S(1)} all-gather(bf16[16,256]{1,0:T(8,128)(2,1)} %param.6), channel_id=1, replica_groups=mesh['row'=32,'col'=32] {'col'}, dimensions={0}, use_global_device_ids=true | all-gather | bytes 270336 | tf_op jit(solution)/shard_map/all_gather | solution.py:36
  101.2 0.1 reshape.26
  101.3 1.5 convert_bitcast_fusion.1
  102.7 2.9 copy.43
  105.6 0.0 copy-done
  105.6 0.0 copy-start.3
  105.6 2.2 convolution_bitcast_fusion.1
  107.8 0.0 copy-done.3
  107.8 3.6 fusion.4
  111.5 1.8 copy.31
  113.3 0.0 copy-start.1
  113.3 2.7 copy.45
  116.0 0.0 reduce-scatter.7.cloned.1.call-update
  116.1 0.0 reduce-scatter.5.cloned.1.call-start
  116.1 135.2 %reduce-scatter.7.cloned.1.call-done = f32[16,896]{1,0:T(8,128)} async-done(((f32[512,896]{1,0:T(8,128)}), f32[16,896]{1,0:T(8,128)}) %reduce-scatter.7.cloned.1.call-update) | async-done | bytes 57360 | tf_op jit(solution)/shard_map/reduce_scatter | solution.py:61
  251.3 0.0 copy-done.1
  251.3 1.5 fusion.24
  252.8 53.7 %all_gather.7 = bf16[512,896]{1,0:T(8,128)(2,1)S(1)} all-gather(bf16[16,896]{1,0:T(8,128)(2,1)S(1)} %get-tuple-element.9), channel_id=1, replica_groups=mesh['row'=32,'col'=32] {'row'}, dimensions={0}, use_global_device_ids=true | all-gather | bytes 946176 | tf_op jit(solution)/shard_map/all_gather | solution.py:65
  306.5 0.5 copy.39
  307.1 1.5 copy.40
  308.5 2.0 convert_bitcast_fusion
  310.6 0.0 copy-start.2
  310.6 0.6 convolution_bitcast_fusion
  311.2 0.0 copy-done.2
  311.2 3.6 fusion
  314.9 0.9 copy.63
  315.8 0.0 reduce-scatter.5.cloned.1.call-update
  315.8 3.3 fusion.13
  319.1 163.5 %reduce-scatter.5.cloned.1.call-done = f32[16,256]{1,0:T(8,128)} async-done(((f32[512,256]{1,0:T(8,128)}), f32[16,256]{1,0:T(8,128)}) %reduce-scatter.5.cloned.1.call-update) | async-done | bytes 16400 | tf_op jit(solution)/shard_map/reduce_scatter | solution.py:83
  482.6 1.3 convert_element_type.40
  (1 shorter events, 0.0 us)
Async XLA Ops:
  7.2 98.4 %copy-start = (bf16[1,1,14,128,128]{4,3,2,1,0:T(8,128)(2,1)S(1)}, bf16[1,1,14,128,128]{4,3,2,1,0:T(8,128)(2,1)}, u32[]{:S(2)}) copy-start(bf16[1,1,14,128,128]{4,3,2,1,0:T(8,128)(2,1)} %param.7) | copy-start | bytes 1376260
  7.2 244.2 %reduce-scatter.7.cloned.1.call-start = ((), (), s32[]{:S(2)}) async-start(), calls=%async_computation.3 | async-start | bytes 1892352 | tf_op jit(solution)/shard_map/reduce_scatter | solution.py:61
  105.6 2.2 copy-start.3
  113.3 138.0 %copy-start.1 = (bf16[16,896]{1,0:T(8,128)(2,1)S(1)}, bf16[16,896]{1,0:T(8,128)(2,1)}, u32[]{:S(2)}) copy-start(bf16[16,896]{1,0:T(8,128)(2,1)} %param.11) | copy-start | bytes 86020
  116.1 366.6 %reduce-scatter.5.cloned.1.call-start = ((), (), s32[]{:S(2)}) async-start(), calls=%async_computation.2 | async-start | bytes 540672 | tf_op jit(solution)/shard_map/reduce_scatter | solution.py:83
  310.6 0.7 copy-start.2
Sparse Core Ops, SparseCore 0:
  116.2 135.1 reduce-scatter.6
  315.9 166.6 reduce-scatter.4
where the time goes:
time: 491 us
  waiting for transfers between devices  299 us (61%)
  blocking collectives  147 us (30%)
  matrix products  16.9 us (3%)
  between operations  14.8 us (3%)
  local copies, waits for them, and re-layouts  10.3 us (2%)
    reduce_scatter x1, waiting for transfers between devices, on_device(): lax.psum_scatter(placed.reshape(rows_here, width_here), 'col', scatter_di...  164 us
    reduce_scatter x1, waiting for transfers between devices, on_device(): lax.psum_scatter(placed.reshape(rows_here, hidden_here), 'row', scatter_d...  135 us
    all_gather x1, blocking collectives, on_device(): gathered = lax.all_gather(tokens, 'col', axis=0, tiled=True)  93.3 us
    all_gather x1, blocking collectives, on_device(): grad_all = lax.all_gather(slope_grad, 'row', axis=0, tiled=True)  53.7 us
  transfers between devices with their start and end apart: 2, of which 2 were waited for; matrix products, arithmetic and copies ran while one was open for 1% of the time, Pallas kernels for 0%

commit v1 on v0

v1 whole, which is shorter than its diff:
```python
import functools

import jax
import jax.numpy as jnp
from jax import lax
from jax.experimental import pallas as pl
from jax.experimental.pallas import tpu as pltpu
from jax.sharding import PartitionSpec as P

MESH = pl.DeviceIdType.MESH
BF16, F32 = jnp.bfloat16, jnp.float32

gelu_scale = 0.7978845608
gelu_cubic = 0.044715

X_LO = 4
X_HI = 2
CORES = 2


def gelu_pair(hidden, cotangent):
    inner = gelu_scale * (hidden + gelu_cubic * hidden * hidden * hidden)
    tangent = jnp.tanh(inner)
    activation = (0.5 * hidden * (1.0 + tangent)).astype(BF16)
    slope = 0.5 * (1.0 + tangent) + 0.5 * hidden * (1.0 - tangent * tangent) * gelu_scale * (
        1.0 + 3.0 * gelu_cubic * hidden * hidden
    )
    return activation, (cotangent.astype(F32) * slope).astype(BF16)


def kernel(
    ring, row_blocks, col_blocks,
    rows_ref, cols_ref, count_ref, tokens_ref, w_ref, gact_ref,
    act_ref, ig_ref, wg_ref,
    tok, dense, half_send, half_recv, half_own, y_send, y_recv, x_send, x_recv,
    gpair, acts, slope, g_full, z_send, z_recv, d_send, d_recv, wg_full,
    ssem, rsem, lsem,
):
    n = ring
    row, col = lax.axis_index("row"), lax.axis_index("col")
    core, x_hi, y = lax.rem(row, CORES), lax.rem(row // CORES, X_HI), row // (CORES * X_HI)
    x_lo, z = lax.rem(col, X_LO), col // X_LO
    slots = w_ref.shape[2]
    block = w_ref.shape[3]
    width, hidden_width = row_blocks * block, col_blocks * block
    slab = tokens_ref.shape[0]
    pair = X_HI * slab

    def at_y(other):
        return ((other * X_HI + x_hi) * CORES + core, col)

    def at_z(other):
        return (row, other * X_LO + x_lo)

    def at_x(other):
        return (row, z * X_LO + other)

    sibling = ((y * X_HI + x_hi) * CORES + 1 - core, col)
    partner = ((y * X_HI + 1 - x_hi) * CORES + core, col)

    def turn(base, step, size):
        return lax.rem(base + step + size, size)

    barrier = pltpu.get_barrier_semaphore()
    peers = [sibling, partner]
    peers += [at_x(turn(x_lo, e, X_LO)) for e in range(1, X_LO)]
    peers += [at_z(turn(z, e, n)) for e in range(1, n)]
    peers += [at_y(turn(y, e, n)) for e in range(1, n)]
    for peer in peers:
        pl.semaphore_signal(barrier, inc=1, device_id=peer, device_id_type=MESH)

    used = [0]

    def numbers(size):
        used[0] += size
        return used[0] - size

    def remote(src, dst, index, peer):
        return pltpu.make_async_remote_copy(
            src_ref=src, dst_ref=dst, send_sem=ssem.at[index], recv_sem=rsem.at[index],
            device_id=peer, device_id_type=MESH,
        )

    my_core, my_pair = lax.rem(x_lo, CORES), x_lo // CORES
    local = [
        pltpu.make_async_copy(tokens_ref, tok.at[z, my_core, my_pair], lsem.at[0]),
        pltpu.make_async_copy(gact_ref, gpair.at[x_hi], lsem.at[1]),
    ]
    for copy in local:
        copy.start()
    pl.semaphore_wait(barrier, len(peers))

    sends = []
    ax = numbers(X_LO)
    for e in range(1, X_LO):
        copy = remote(tokens_ref, tok.at[z, my_core, my_pair], ax + e, at_x(turn(x_lo, e, X_LO)))
        copy.start()
        sends.append(copy)
    gp = numbers(1)
    gp_copy = remote(gact_ref, gpair.at[x_hi], gp, partner)
    gp_copy.start()
    sends.append(gp_copy)

    count = count_ref[0, 0]
    places = [rows_ref[0, 0, s] * col_blocks + cols_ref[0, 0, s] for s in range(slots)]
    for p in range(row_blocks * col_blocks):
        slot = jnp.int32(0)
        for s in range(slots):
            slot = jnp.where(places[s] == p, s, slot)
        live = jnp.where(slot < count, 1, 0).astype(F32)
        r, c = p // col_blocks, p % col_blocks
        dense[r * block:(r + 1) * block, c * block:(c + 1) * block] = (
            w_ref[0, 0, slot].astype(F32) * live
        ).astype(BF16)

    for copy in local:
        copy.wait()
    for e in range(1, X_LO):
        source = turn(x_lo, -e, X_LO)
        remote(
            tokens_ref, tok.at[z, lax.rem(source, CORES), source // CORES], ax + e,
            at_x(turn(x_lo, e, X_LO)),
        ).wait_recv()
    far_first = sorted(range(1, n), key=lambda d: (-min(d, n - d), d))
    near_first = far_first[::-1]
    az = numbers(n)
    for d in far_first:
        copy = remote(tok.at[z], tok.at[z], az + d, at_z(turn(z, d, n)))
        copy.start()
        sends.append(copy)
    for d in near_first:
        source = turn(z, -d, n)
        remote(tok.at[source], tok.at[source], az + d, at_z(turn(z, d, n))).wait_recv()

    order = far_first + [0]
    b1 = numbers(2)
    cuts = [(0, n // 2), (n // 2, n)]
    b1_copies = []

    def product(which, low, high):
        lhs = jnp.concatenate(
            [tok[turn(y, d, n), which].reshape(pair, width) for d in order[low:high]], axis=0
        )
        return jnp.dot(lhs, dense[...], preferred_element_type=F32).reshape(
            high - low, pair, hidden_width
        )

    for i, (low, high) in enumerate(cuts):
        half_send[low:high] = product(1 - core, low, high)
        copy = remote(half_send.at[pl.ds(low, high - low)], half_recv.at[pl.ds(low, high - low)], b1 + i, sibling)
        copy.start()
        b1_copies.append(copy)
        sends.append(copy)
    for low, high in cuts:
        half_own[low:high] = product(core, low, high)
    b2 = numbers(n)
    y_copies = {}
    for i, (low, high) in enumerate(cuts):
        b1_copies[i].wait_recv()
        for at in range(low, high):
            d = order[at]
            if d:
                y_send[at] = (half_own[at] + half_recv[at]).astype(BF16)
                y_copies[d] = remote(y_send.at[at], y_recv.at[d], b2 + d, at_y(turn(y, d, n)))
                y_copies[d].start()
                sends.append(y_copies[d])
    total = half_own[n - 1] + half_recv[n - 1]
    for d in near_first:
        y_copies[d].wait_recv()
        total = total + y_recv[d].astype(F32)
    b3 = numbers(1)
    x_send[...] = total.astype(BF16)
    x_copy = remote(x_send, x_recv, b3, partner)
    x_copy.start()
    sends.append(x_copy)
    half_own[0] = total
    x_copy.wait_recv()
    gp_copy.wait_recv()
    hidden = half_own[0] + x_recv[...].astype(F32)
    activation, grad = gelu_pair(hidden, gpair[...].reshape(pair, hidden_width))
    acts[...] = activation.reshape(X_HI, slab, hidden_width)
    slope[y, core] = grad.reshape(X_HI, slab, hidden_width)

    c2, c3 = numbers(n), numbers(n)
    for d in far_first:
        copy = remote(slope.at[y, core], slope.at[y, core], c2 + d, at_y(turn(y, d, n)))
        copy.start()
        sends.append(copy)
    copy = remote(slope.at[y, core], slope.at[y, core], c3, sibling)
    copy.start()
    sends.append(copy)
    act_ref[...] = acts[x_hi]

    d1 = numbers(n)

    def to_z(to):
        return pltpu.make_async_remote_copy(
            src_ref=z_send.at[to], dst_ref=z_recv.at[z], send_sem=ssem.at[d1 + to],
            recv_sem=rsem.at[d1 + z], device_id=at_z(to), device_id_type=MESH,
        )

    def input_part(d):
        source = turn(y, -d, n)
        remote(slope.at[source, 1 - core], slope.at[source, 1 - core], c3 + d, sibling).wait_recv()
        lhs = slope[source].reshape(CORES * pair, hidden_width)
        part = lax.dot_general(
            lhs, dense[...], (((1,), (1,)), ((), ())), preferred_element_type=F32
        )
        g_full[source] = part
        z_send[source] = part.astype(BF16).reshape(CORES * pair, width)

        @pl.when(source != z)
        def _():
            to_z(source).start()

    waiting = [0]
    for d in near_first:
        source = turn(y, -d, n)
        remote(slope.at[source, core], slope.at[source, core], c2 + d, at_y(turn(y, d, n))).wait_recv()
        copy = remote(slope.at[source, core], slope.at[source, core], c3 + d, sibling)
        copy.start()
        sends.append(copy)
        input_part(waiting[0])
        waiting[0] = d
    input_part(waiting[0])

    all_tokens = tok[...].reshape(n * CORES * pair, width)
    all_slopes = slope[...].reshape(n * CORES * pair, hidden_width)
    full = lax.dot_general(
        all_tokens, all_slopes, (((0,), (0,)), ((), ())), preferred_element_type=F32
    )
    for p in range(row_blocks * col_blocks):
        r, c = p // col_blocks, p % col_blocks
        wg_full[p] = full[r * block:(r + 1) * block, c * block:(c + 1) * block]
    for s in range(slots):
        live = jnp.where(s < count, 1, 0).astype(F32)
        wg_ref[0, 0, s] = (wg_full[places[s]] * live).astype(BF16)

    total = g_full[z]
    for e in near_first:
        source = turn(z, -e, n)
        pltpu.make_async_remote_copy(
            src_ref=z_send.at[source], dst_ref=z_recv.at[source], send_sem=ssem.at[d1 + source],
            recv_sem=rsem.at[d1 + source], device_id=at_z(source), device_id_type=MESH,
        ).wait_recv()
        total = total + z_recv[source].astype(F32)
    d_send[...] = total.reshape(CORES, X_HI, slab, width)
    d2 = numbers(X_LO)
    d_copies = []
    for e in range(1, X_LO):
        to = turn(x_lo, e, X_LO)
        copy = remote(d_send.at[lax.rem(to, CORES), to // CORES], d_recv.at[e], d2 + e, at_x(to))
        copy.start()
        d_copies.append(copy)
        sends.append(copy)
    result = d_send[my_core, my_pair]
    for e in range(1, X_LO):
        d_copies[e - 1].wait_recv()
        result = result + d_recv[e]
    ig_ref[...] = result.astype(BF16)

    for copy in sends:
        copy.wait_send()
    for e in range(1, n):
        to_z(turn(z, e, n)).wait_send()


def on_device(ring, tokens, w_packed, kept_rows, kept_cols, kept_count, grad_act):
    n = ring
    block, slots = w_packed.shape[-1], w_packed.shape[2]
    slab, width = tokens.shape
    hidden_width = grad_act.shape[1]
    row_blocks, col_blocks = width // block, hidden_width // block
    pair = X_HI * slab
    sems = 3 * X_LO + 2 + 2 + 6 * n
    vmem, smem = pl.BlockSpec(memory_space=pltpu.VMEM), pl.BlockSpec(memory_space=pltpu.SMEM)
    return tuple(pl.pallas_call(
        functools.partial(kernel, n, row_blocks, col_blocks),
        out_shape=(
            jax.ShapeDtypeStruct(grad_act.shape, BF16),
            jax.ShapeDtypeStruct(tokens.shape, BF16),
            jax.ShapeDtypeStruct(w_packed.shape, BF16),
        ),
        in_specs=[smem, smem, smem, vmem, vmem, vmem],
        out_specs=(vmem, vmem, vmem),
        scratch_shapes=[
            pltpu.VMEM((n, CORES, X_HI, slab, width), BF16),
            pltpu.VMEM((width, hidden_width), BF16),
            pltpu.VMEM((n, pair, hidden_width), F32),
            pltpu.VMEM((n, pair, hidden_width), F32),
            pltpu.VMEM((n, pair, hidden_width), F32),
            pltpu.VMEM((n, pair, hidden_width), BF16),
            pltpu.VMEM((n, pair, hidden_width), BF16),
            pltpu.VMEM((pair, hidden_width), BF16),
            pltpu.VMEM((pair, hidden_width), BF16),
            pltpu.VMEM((X_HI, slab, hidden_width), BF16),
            pltpu.VMEM((X_HI, slab, hidden_width), BF16),
            pltpu.VMEM((n, CORES, X_HI, slab, hidden_width), BF16),
            pltpu.VMEM((n, CORES * pair, width), F32),
            pltpu.VMEM((n, CORES * pair, width), BF16),
            pltpu.VMEM((n, CORES * pair, width), BF16),
            pltpu.VMEM((CORES, X_HI, slab, width), F32),
            pltpu.VMEM((X_LO, slab, width), F32),
            pltpu.VMEM((row_blocks * col_blocks, block, block), F32),
            pltpu.SemaphoreType.DMA((sems,)),
            pltpu.SemaphoreType.DMA((sems,)),
            pltpu.SemaphoreType.DMA((2,)),
        ],
        compiler_params=pltpu.CompilerParams(collective_id=0, has_side_effects=True),
    )(kept_rows, kept_cols, kept_count, tokens, w_packed, grad_act))


def solution(mesh):
    ring = mesh.shape["row"] // (CORES * X_HI)
    placed = (
        P("col", "row"),
        P("row", "col", None, None, None),
        P("row", "col", None),
        P("row", "col", None),
        P("row", "col"),
        P("row", "col"),
    )
    return jax.shard_map(
        functools.partial(on_device, ring),
        mesh=mesh,
        in_specs=placed,
        out_specs=(P("row", "col"), P("col", "row"), P("row", "col", None, None, None)),
        check_vma=False,
    )
```

time: 491 us -> 86.8 us (0.18)
  the two profiles are of different devices: /device:TPU:16 before, /device:TPU:49 now
where the time goes in v1:
time: 86.8 us; the launch traced here: 86.5 us
  Pallas kernels  81.4 us (94%)
  local copies, waits for them, and re-layouts  3.79 us (4%)
  between operations  1.3 us (1%)
    pallas_call x1, Pallas kernels, on_device(): pl.pallas_call(functools.partial(kernel, n, row_blocks, col_blocks), out_...  81.4 us
    unnamed x5, local copies, waits for them, and re-layouts  3.79 us

profile of v1, /device:TPU:49, one launch (start us, length us, event | category | flops | bytes accessed | tf_op | source)
XLA Modules:
  0.0 86.5 jit_solution(18196243242641793223)
XLA Ops:
  1.3 81.4 %shard_map.85 = (bf16[16,896]{1,0:T(8,128)(2,1)}, bf16[16,256]{1,0:T(8,128)(2,1)}, bf16[1,1,14,128,128]{4,3,2,1,0:T(8,128)(2,1)}) custom-call(s32[1,1,14]{2,1,0:T(1,128)} %rows_ref.1, s32[1,1,14]{2,1,0:T(1,128)} %cols_ref.1, s32[1,1]{1,0:T(1,128)S(6)} %copy.12.count_ref, bf16[16,256]{1,0:T(8,128)(2,1)} %tokens_ref.1, bf16[1,1,14,128,128]{4,3,2,1,0:T(8,128)(2,1)} %w_ref.1, ...), custom_call_target="tpu_custom_call" | custom-call | tf_op jit(solution)/shard_map/pallas_call | solution.py:277
  82.7 0.0 copy-start
  82.7 1.4 %copy.13 = bf16[16,896]{1,0:T(8,128)(2,1)} copy(bf16[16,896]{1,0:T(8,128)(2,1)} %get-tuple-element.6) | data formatting | bytes 57344
  84.1 0.0 copy-done
  84.1 0.6 copy.14
  84.7 1.8 %copy.15 = bf16[1,1,14,128,128]{4,3,2,1,0:T(8,128)(2,1)} copy(bf16[1,1,14,128,128]{4,3,2,1,0:T(8,128)(2,1)} %get-tuple-element.8) | data formatting | bytes 917504
Async XLA Ops:
  82.7 1.4 %copy-start = (bf16[16,256]{1,0:T(8,128)(2,1)S(1)}, bf16[16,256]{1,0:T(8,128)(2,1)}, u32[]{:S(2)}) copy-start(bf16[16,256]{1,0:T(8,128)(2,1)} %get-tuple-element.7) | copy-start | bytes 24580

commit v2 on v1

v2 whole, which is shorter than its diff:
```python
import functools

import jax
import jax.numpy as jnp
from jax import lax
from jax.experimental import pallas as pl
from jax.experimental.pallas import tpu as pltpu
from jax.sharding import PartitionSpec as P

MESH = pl.DeviceIdType.MESH
BF16, F32 = jnp.bfloat16, jnp.float32

gelu_scale = 0.7978845608
gelu_cubic = 0.044715

X_LO = 4
X_HI = 2
CORES = 2


def gelu_pair(hidden, cotangent):
    inner = gelu_scale * (hidden + gelu_cubic * hidden * hidden * hidden)
    tangent = jnp.tanh(inner)
    activation = (0.5 * hidden * (1.0 + tangent)).astype(BF16)
    slope = 0.5 * (1.0 + tangent) + 0.5 * hidden * (1.0 - tangent * tangent) * gelu_scale * (
        1.0 + 3.0 * gelu_cubic * hidden * hidden
    )
    return activation, (cotangent.astype(F32) * slope).astype(BF16)


def kernel(
    ring, row_blocks, col_blocks, cuts,
    rows_ref, cols_ref, count_hbm, tokens_ref, w_hbm, gact_ref,
    act_ref, ig_ref, wg_ref,
    tok, dense, w_ref, gpair, acts, g_full, z_send, z_recv, d_send, d_recv, wg_full, count_ref,
    ssem, rsem, lsem, *per_cut,
):
    n = ring
    part, sib, own, y_send, y_recv, x_send, x_recv, slope = (
        per_cut[i * len(cuts):(i + 1) * len(cuts)] for i in range(8)
    )
    row, col = lax.axis_index("row"), lax.axis_index("col")
    core, x_hi, y = lax.rem(row, CORES), lax.rem(row // CORES, X_HI), row // (CORES * X_HI)
    x_lo, z = lax.rem(col, X_LO), col // X_LO
    slots, block = w_ref.shape[0], w_ref.shape[1]
    width = row_blocks * block
    slab = tokens_ref.shape[0]
    pair = X_HI * slab

    def at_y(other):
        return ((other * X_HI + x_hi) * CORES + core, col)

    def at_z(other):
        return (row, other * X_LO + x_lo)

    def at_x(other):
        return (row, z * X_LO + other)

    sibling = ((y * X_HI + x_hi) * CORES + 1 - core, col)
    partner = ((y * X_HI + 1 - x_hi) * CORES + core, col)

    def turn(base, step, size):
        return lax.rem(base + step + size, size)

    barrier = pltpu.get_barrier_semaphore()
    peers = [sibling, partner]
    peers += [at_x(turn(x_lo, e, X_LO)) for e in range(1, X_LO)]
    peers += [at_z(turn(z, e, n)) for e in range(1, n)]
    peers += [at_y(turn(y, e, n)) for e in range(1, n)]
    for peer in peers:
        pl.semaphore_signal(barrier, inc=1, device_id=peer, device_id_type=MESH)

    used = [0]

    def numbers(size):
        used[0] += size
        return used[0] - size

    def remote(src, dst, send, receive, peer):
        return pltpu.make_async_remote_copy(
            src_ref=src, dst_ref=dst, send_sem=ssem.at[send], recv_sem=rsem.at[receive],
            device_id=peer, device_id_type=MESH,
        )

    steps = [i // 2 + (i % 2) * (n // 2) for i in range(n)]

    def piece(o):
        return lax.rem(y + z + o, n)

    def y_other(o):
        return lax.rem(y - z - o + 2 * n, n)

    def z_other(o):
        return lax.rem(z - y - o + 2 * n, n)

    my_core, my_pair = lax.rem(x_lo, CORES), x_lo // CORES
    mine = tok.at[z, my_core, my_pair]
    local = [
        pltpu.make_async_copy(tokens_ref, mine, lsem.at[0]),
        pltpu.make_async_copy(w_hbm.at[0, 0], w_ref, lsem.at[1]),
        pltpu.make_async_copy(count_hbm, count_ref, lsem.at[2]),
        pltpu.make_async_copy(gact_ref, gpair.at[x_hi], lsem.at[3]),
    ]
    for copy in local:
        copy.start()
    local[0].wait()
    pl.semaphore_wait(barrier, len(peers))

    sends = []
    ax = numbers(X_LO)
    for e in range(1, X_LO):
        copy = remote(mine, mine, ax + e, ax + e, at_x(turn(x_lo, e, X_LO)))
        copy.start()
        sends.append(copy)

    for copy in local[1:]:
        copy.wait()
    gp = numbers(1)
    gp_copy = remote(gpair.at[x_hi], gpair.at[x_hi], gp, gp, partner)
    gp_copy.start()
    sends.append(gp_copy)
    count = count_ref[0, 0]
    places = [rows_ref[0, 0, s] * col_blocks + cols_ref[0, 0, s] for s in range(slots)]
    for p in range(row_blocks * col_blocks):
        slot = jnp.int32(0)
        for s in range(slots):
            slot = jnp.where(places[s] == p, s, slot)
        live = jnp.where(slot < count, 1, 0).astype(F32)
        r, c = p // col_blocks, p % col_blocks
        dense[r * block:(r + 1) * block, c * block:(c + 1) * block] = (
            w_ref[slot].astype(F32) * live
        ).astype(BF16)

    for e in range(1, X_LO):
        source = turn(x_lo, -e, X_LO)
        theirs = tok.at[z, lax.rem(source, CORES), source // CORES]
        remote(theirs, theirs, ax + e, ax + e, at_x(source)).wait_recv()
    az = numbers(n)
    for o in steps:
        to = z_other(o)

        @pl.when(to != z)
        def _():
            remote(tok.at[z], tok.at[z], az + to, az + z, at_z(to)).start()

    b1 = [numbers(n) for _ in cuts]
    b2 = [numbers(n) for _ in cuts]
    b3 = [numbers(1) for _ in cuts]
    c2 = [numbers(n) for _ in cuts]
    c3 = [numbers(n) for _ in cuts]
    d1, d2 = numbers(n), numbers(X_LO)

    def half_copy(h, i):
        return remote(part[h].at[i, 1 - core], sib[h].at[i], b1[h] + i, b1[h] + i, sibling)

    def y_copy(h, i, to):
        return remote(y_send[h].at[i], y_recv[h].at[y], b2[h] + to, b2[h] + y, at_y(to))

    def multiply(h, i):
        low, high = cuts[h]
        j = piece(steps[i])
        if h == 0:
            @pl.when(j != z)
            def _():
                remote(tok.at[j], tok.at[j], az + j, az + j, at_z(j)).wait_recv()
        product = jnp.dot(
            tok[j].reshape(CORES * pair, width), dense[:, low:high], preferred_element_type=F32
        )
        part[h][i] = product.reshape(CORES, pair, high - low)
        half_copy(h, i).start()

    def pass_on(h, i):
        j = piece(steps[i])
        half_copy(h, i).wait_recv()
        both = part[h][i, core] + sib[h][i]
        y_send[h][i] = both.astype(BF16)

        @pl.when(j == y)
        def _():
            own[h][...] = both

        @pl.when(j != y)
        def _():
            y_copy(h, i, j).start()

    before = None
    for h in range(len(cuts)):
        for i in range(n):
            multiply(h, i)
            if before is not None:
                pass_on(*before)
            before = (h, i)
    pass_on(*before)

    for h, (low, high) in enumerate(cuts):
        for o in steps:
            source = y_other(o)

            @pl.when(source != y)
            def _():
                remote(
                    y_send[h].at[0], y_recv[h].at[source], b2[h] + source, b2[h] + source, at_y(source)
                ).wait_recv()
                own[h][...] += y_recv[h][source].astype(F32)

        x_send[h][...] = own[h][...].astype(BF16)
        x_copy = remote(x_send[h], x_recv[h], b3[h], b3[h], partner)
        x_copy.start()
        sends.append(x_copy)
        x_copy.wait_recv()
        if h == 0:
            gp_copy.wait_recv()
        hidden = own[h][...] + x_recv[h][...].astype(F32)
        activation, grad = gelu_pair(hidden, gpair[:, :, low:high].reshape(pair, high - low))
        acts[:, :, low:high] = activation.reshape(X_HI, slab, high - low)
        slope[h][y, core] = grad.reshape(X_HI, slab, high - low)

        for o in steps:
            to = y_other(o)

            @pl.when(to != y)
            def _():
                here = slope[h].at[y, core]
                remote(here, here, c2[h] + to, c2[h] + y, at_y(to)).start()

        here = slope[h].at[y, core]
        remote(here, here, c3[h] + y, c3[h] + y, sibling).start()
    act_ref[...] = acts[x_hi]

    def z_copy(to):
        return remote(z_send.at[to], z_recv.at[z], d1 + to, d1 + z, at_z(to))

    def relay(h, i):
        j = piece(steps[i])

        @pl.when(j != y)
        def _():
            there = slope[h].at[j, core]
            remote(there, there, c2[h] + j, c2[h] + j, at_y(j)).wait_recv()
            remote(there, there, c3[h] + j, c3[h] + j, sibling).start()

    def input_part(h, i):
        low, high = cuts[h]
        j = piece(steps[i])
        there = slope[h].at[j, 1 - core]
        remote(there, there, c3[h] + j, c3[h] + j, sibling).wait_recv()
        share = lax.dot_general(
            slope[h][j].reshape(CORES * pair, high - low), dense[:, low:high],
            (((1,), (1,)), ((), ())), preferred_element_type=F32,
        )
        if h:
            share = share + g_full[j]
        g_full[j] = share
        if h == len(cuts) - 1:
            z_send[j] = share.astype(BF16)

            @pl.when(j != z)
            def _():
                z_copy(j).start()

    before = None
    for h in range(len(cuts)):
        for i in range(n):
            relay(h, i)
            if before is not None:
                input_part(*before)
            before = (h, i)
    input_part(*before)

    all_tokens = tok[...].reshape(n * CORES * pair, width)
    for h, (low, high) in enumerate(cuts):
        full = lax.dot_general(
            all_tokens, slope[h][...].reshape(n * CORES * pair, high - low),
            (((0,), (0,)), ((), ())), preferred_element_type=F32,
        )
        for r in range(row_blocks):
            for c in range(low // block, high // block):
                wg_full[r * col_blocks + c] = full[
                    r * block:(r + 1) * block, c * block - low:(c + 1) * block - low
                ]
    for s in range(slots):
        live = jnp.where(s < count, 1, 0).astype(F32)
        wg_ref[0, 0, s] = (wg_full[places[s]] * live).astype(BF16)

    d_send[...] = g_full[z].reshape(CORES, X_HI, slab, width)
    for o in steps:
        source = z_other(o)

        @pl.when(source != z)
        def _():
            remote(z_send.at[0], z_recv.at[source], d1 + source, d1 + source, at_z(source)).wait_recv()
            d_send[...] += z_recv[source].astype(F32).reshape(CORES, X_HI, slab, width)

    d_copies = []
    for e in range(1, X_LO):
        to = turn(x_lo, e, X_LO)
        copy = remote(d_send.at[lax.rem(to, CORES), to // CORES], d_recv.at[e], d2 + e, d2 + e, at_x(to))
        copy.start()
        d_copies.append(copy)
        sends.append(copy)
    result = d_send[my_core, my_pair]
    for e in range(1, X_LO):
        d_copies[e - 1].wait_recv()
        result = result + d_recv[e]
    ig_ref[...] = result.astype(BF16)

    for copy in sends:
        copy.wait_send()
    for e in range(1, n):
        to = turn(z, e, n)
        remote(tok.at[z], tok.at[z], az + to, az + z, at_z(to)).wait_send()
        z_copy(to).wait_send()
        to = turn(y, e, n)
        for h in range(len(cuts)):
            y_copy(h, 0, to).wait_send()
            here = slope[h].at[y, core]
            remote(here, here, c2[h] + to, c2[h] + y, at_y(to)).wait_send()
    for h in range(len(cuts)):
        for i in range(n):
            half_copy(h, i).wait_send()
            there = slope[h].at[i, core]
            remote(there, there, c3[h] + i, c3[h] + i, sibling).wait_send()


def on_device(ring, tokens, w_packed, kept_rows, kept_cols, kept_count, grad_act):
    n = ring
    block, slots = w_packed.shape[-1], w_packed.shape[2]
    slab, width = tokens.shape
    hidden_width = grad_act.shape[1]
    row_blocks, col_blocks = width // block, hidden_width // block
    pair = X_HI * slab
    middle = (col_blocks + 1) // 2 * block
    cuts = ((0, middle), (middle, hidden_width))
    sems = 2 * X_LO + 1 + 2 * n + len(cuts) * (4 * n + 1)
    vmem, smem = pl.BlockSpec(memory_space=pltpu.VMEM), pl.BlockSpec(memory_space=pltpu.SMEM)
    hbm = pl.BlockSpec(memory_space=pltpu.HBM)

    def each(lead, kind):
        return [pltpu.VMEM(lead + (high - low,), kind) for low, high in cuts]

    return tuple(pl.pallas_call(
        functools.partial(kernel, n, row_blocks, col_blocks, cuts),
        out_shape=(
            jax.ShapeDtypeStruct(grad_act.shape, BF16),
            jax.ShapeDtypeStruct(tokens.shape, BF16),
            jax.ShapeDtypeStruct(w_packed.shape, BF16),
        ),
        in_specs=[smem, smem, hbm, hbm, hbm, hbm],
        out_specs=(vmem, vmem, vmem),
        scratch_shapes=[
            pltpu.VMEM((n, CORES, X_HI, slab, width), BF16),
            pltpu.VMEM((width, hidden_width), BF16),
            pltpu.VMEM((slots, block, block), BF16),
            pltpu.VMEM((X_HI, slab, hidden_width), BF16),
            pltpu.VMEM((X_HI, slab, hidden_width), BF16),
            pltpu.VMEM((n, CORES * pair, width), F32),
            pltpu.VMEM((n, CORES * pair, width), BF16),
            pltpu.VMEM((n, CORES * pair, width), BF16),
            pltpu.VMEM((CORES, X_HI, slab, width), F32),
            pltpu.VMEM((X_LO, slab, width), F32),
            pltpu.VMEM((row_blocks * col_blocks, block, block), F32),
            pltpu.SMEM((1, 1), jnp.int32),
            pltpu.SemaphoreType.DMA((sems,)),
            pltpu.SemaphoreType.DMA((sems,)),
            pltpu.SemaphoreType.DMA((4,)),
            *each((n, CORES, pair), F32),
            *each((n, pair), F32),
            *each((pair,), F32),
            *each((n, pair), BF16),
            *each((n, pair), BF16),
            *each((pair,), BF16),
            *each((pair,), BF16),
            *each((n, CORES, X_HI, slab), BF16),
        ],
        compiler_params=pltpu.CompilerParams(
            collective_id=0, has_side_effects=True, vmem_limit_bytes=24 << 20
        ),
    )(kept_rows, kept_cols, kept_count, tokens, w_packed, grad_act))


def solution(mesh):
    ring = mesh.shape["row"] // (CORES * X_HI)
    placed = (
        P("col", "row"),
        P("row", "col", None, None, None),
        P("row", "col", None),
        P("row", "col", None),
        P("row", "col"),
        P("row", "col"),
    )
    return jax.shard_map(
        functools.partial(on_device, ring),
        mesh=mesh,
        in_specs=placed,
        out_specs=(P("row", "col"), P("col", "row"), P("row", "col", None, None, None)),
        check_vma=False,
    )
```

time: 86.8 us -> 81 us (0.933)
  the two profiles are of different devices: /device:TPU:49 before, /device:TPU:1 now
where the time goes in v2:
time: 81 us; the launch traced here: 80.7 us
  Pallas kernels  74.9 us (92%)
  local copies, waits for them, and re-layouts  4.44 us (5%)
  between operations  1.35 us (2%)
    pallas_call x1, Pallas kernels, on_device(): pl.pallas_call(functools.partial(kernel, n, row_blocks, col_blocks, cuts)...  74.9 us
    unnamed x13, local copies, waits for them, and re-layouts  4.44 us

profile of v2, /device:TPU:1, one launch (start us, length us, event | category | flops | bytes accessed | tf_op | source)
XLA Modules:
  0.0 80.7 jit_solution(17982187894769461151)
XLA Ops:
  0.6 0.0 copy-start.4
  0.6 0.0 copy-start.3
  1.3 0.0 copy-done.4
  1.3 0.0 copy-done.3
  1.3 0.0 copy-start
  1.3 1.0 %copy-done = bf16[1,1,14,128,128]{4,3,2,1,0:T(8,128)(2,1)S(1)} copy-done((bf16[1,1,14,128,128]{4,3,2,1,0:T(8,128)(2,1)S(1)}, bf16[1,1,14,128,128]{4,3,2,1,0:T(8,128)(2,1)}, u32[]{:S(2)}) %copy-start) | copy-done | bytes 458776
  2.4 0.0 copy-start.1
  2.4 0.7 copy-done.1
  3.1 0.0 copy-start.2
  3.1 0.7 copy-done.2
  3.8 74.9 %shard_map.85 = (bf16[16,896]{1,0:T(8,128)(2,1)S(1)}, bf16[16,256]{1,0:T(8,128)(2,1)S(1)}, bf16[1,1,14,128,128]{4,3,2,1,0:T(8,128)(2,1)S(1)}) custom-call(s32[1,1,14]{2,1,0:T(1,128)S(1)} %copy-done.3, s32[1,1,14]{2,1,0:T(1,128)S(1)} %copy-done.4, s32[1,1]{1,0:T(1,128)S(6)} %copy.12.count_hbm, bf16[16,256]{1,0:T(8,128)(2,1)S(1)} %copy-done.2, ...), custom_call_target="tpu_custom_call" | custom-call | tf_op jit(solution)/shard_map/pallas_call | solution.py:341
  78.7 0.6 copy.13
  79.3 0.6 copy.14
  79.9 0.8 copy.15
Async XLA Ops:
  0.6 0.7 copy-start.4
  0.6 0.7 copy-start.3
  1.3 1.0 %copy-start = (bf16[1,1,14,128,128]{4,3,2,1,0:T(8,128)(2,1)S(1)}, bf16[1,1,14,128,128]{4,3,2,1,0:T(8,128)(2,1)}, u32[]{:S(2)}) copy-start(bf16[1,1,14,128,128]{4,3,2,1,0:T(8,128)(2,1)} %w_hbm.1) | copy-start | bytes 1376260
  2.4 0.7 copy-start.1
  3.1 0.7 copy-start.2

commit v3 on v2

--- a/solution.py
+++ b/solution.py
@@ -32,7 +32,7 @@
     ring, row_blocks, col_blocks, cuts,
     rows_ref, cols_ref, count_hbm, tokens_ref, w_hbm, gact_ref,
     act_ref, ig_ref, wg_ref,
-    tok, dense, w_ref, gpair, acts, g_full, z_send, z_recv, d_send, d_recv, wg_full, count_ref,
+    tok, dense, dense_t, w_ref, gpair, acts, g_full, z_send, z_recv, d_send, d_recv, wg_full, w_grad, in_grad, count_ref,
     ssem, rsem, lsem, *per_cut,
 ):
     n = ring
@@ -130,6 +130,9 @@
         dense[r * block:(r + 1) * block, c * block:(c + 1) * block] = (
             w_ref[slot].astype(F32) * live
         ).astype(BF16)
+        dense_t[c * block:(c + 1) * block, r * block:(r + 1) * block] = jnp.transpose(
+            w_ref[slot].astype(F32) * live
+        ).astype(BF16)
 
     for e in range(1, X_LO):
         source = turn(x_lo, -e, X_LO)
@@ -225,13 +228,19 @@
 
         here = slope[h].at[y, core]
         remote(here, here, c3[h] + y, c3[h] + y, sibling).start()
-    act_ref[...] = acts[x_hi]
+    out_act = pltpu.make_async_copy(acts.at[x_hi], act_ref, lsem.at[4])
+    out_act.start()
 
     def z_copy(to):
         return remote(z_send.at[to], z_recv.at[z], d1 + to, d1 + z, at_z(to))
 
+    near_first = sorted(range(n), key=lambda d: (min(d, n - d), d))
+
+    def arrival(h, i):
+        return turn(y, -near_first[i], n)
+
     def relay(h, i):
-        j = piece(steps[i])
+        j = arrival(h, i)
 
         @pl.when(j != y)
         def _():
@@ -241,12 +250,11 @@
 
     def input_part(h, i):
         low, high = cuts[h]
-        j = piece(steps[i])
+        j = arrival(h, i)
         there = slope[h].at[j, 1 - core]
         remote(there, there, c3[h] + j, c3[h] + j, sibling).wait_recv()
-        share = lax.dot_general(
-            slope[h][j].reshape(CORES * pair, high - low), dense[:, low:high],
-            (((1,), (1,)), ((), ())), preferred_element_type=F32,
+        share = jnp.dot(
+            slope[h][j].reshape(CORES * pair, high - low), dense_t[low:high], preferred_element_type=F32
         )
         if h:
             share = share + g_full[j]
@@ -280,7 +288,9 @@
                 ]
     for s in range(slots):
         live = jnp.where(s < count, 1, 0).astype(F32)
-        wg_ref[0, 0, s] = (wg_full[places[s]] * live).astype(BF16)
+        w_grad[s] = (wg_full[places[s]] * live).astype(BF16)
+    out_wg = pltpu.make_async_copy(w_grad, wg_ref.at[0, 0], lsem.at[5])
+    out_wg.start()
 
     d_send[...] = g_full[z].reshape(CORES, X_HI, slab, width)
     for o in steps:
@@ -302,7 +312,11 @@
     for e in range(1, X_LO):
         d_copies[e - 1].wait_recv()
         result = result + d_recv[e]
-    ig_ref[...] = result.astype(BF16)
+    in_grad[...] = result.astype(BF16)
+    out_ig = pltpu.make_async_copy(in_grad, ig_ref, lsem.at[6])
+    out_ig.start()
+    for copy in (out_act, out_wg, out_ig):
+        copy.wait()
 
     for copy in sends:
         copy.wait_send()
@@ -322,6 +336,18 @@
             remote(there, there, c3[h] + i, c3[h] + i, sibling).wait_send()
 
 
+def store(act_ref, ig_ref, wg_ref, act_out, ig_out, wg_out, sem):
+    copies = [
+        pltpu.make_async_copy(wg_ref, wg_out, sem.at[0]),
+        pltpu.make_async_copy(act_ref, act_out, sem.at[1]),
+        pltpu.make_async_copy(ig_ref, ig_out, sem.at[2]),
+    ]
+    for copy in copies:
+        copy.start()
+    for copy in copies:
+        copy.wait()
+
+
 def on_device(ring, tokens, w_packed, kept_rows, kept_cols, kept_count, grad_act):
     n = ring
     block, slots = w_packed.shape[-1], w_packed.shape[2]
@@ -338,7 +364,7 @@
     def each(lead, kind):
         return [pltpu.VMEM(lead + (high - low,), kind) for low, high in cuts]
 
-    return tuple(pl.pallas_call(
+    results = pl.pallas_call(
         functools.partial(kernel, n, row_blocks, col_blocks, cuts),
         out_shape=(
             jax.ShapeDtypeStruct(grad_act.shape, BF16),
@@ -346,10 +372,11 @@
             jax.ShapeDtypeStruct(w_packed.shape, BF16),
         ),
         in_specs=[smem, smem, hbm, hbm, hbm, hbm],
-        out_specs=(vmem, vmem, vmem),
+        out_specs=(hbm, hbm, hbm),
         scratch_shapes=[
             pltpu.VMEM((n, CORES, X_HI, slab, width), BF16),
             pltpu.VMEM((width, hidden_width), BF16),
+            pltpu.VMEM((hidden_width, width), BF16),
             pltpu.VMEM((slots, block, block), BF16),
             pltpu.VMEM((X_HI, slab, hidden_width), BF16),
             pltpu.VMEM((X_HI, slab, hidden_width), BF16),
@@ -359,10 +386,12 @@
             pltpu.VMEM((CORES, X_HI, slab, width), F32),
             pltpu.VMEM((X_LO, slab, width), F32),
             pltpu.VMEM((row_blocks * col_blocks, block, block), F32),
+            pltpu.VMEM((slots, block, block), BF16),
+            pltpu.VMEM((slab, width), BF16),
             pltpu.SMEM((1, 1), jnp.int32),
             pltpu.SemaphoreType.DMA((sems,)),
             pltpu.SemaphoreType.DMA((sems,)),
-            pltpu.SemaphoreType.DMA((4,)),
+            pltpu.SemaphoreType.DMA((7,)),
             *each((n, CORES, pair), F32),
             *each((n, pair), F32),
             *each((pair,), F32),
@@ -373,9 +402,16 @@
             *each((n, CORES, X_HI, slab), BF16),
         ],
         compiler_params=pltpu.CompilerParams(
-            collective_id=0, has_side_effects=True, vmem_limit_bytes=24 << 20
+            collective_id=0, has_side_effects=True
         ),
-    )(kept_rows, kept_cols, kept_count, tokens, w_packed, grad_act))
+    )(kept_rows, kept_cols, kept_count, tokens, w_packed, grad_act)
+    return tuple(pl.pallas_call(
+        store,
+        out_shape=tuple(jax.ShapeDtypeStruct(r.shape, r.dtype) for r in results),
+        in_specs=[vmem] * 3,
+        out_specs=(hbm,) * 3,
+        scratch_shapes=[pltpu.SemaphoreType.DMA((3,))],
+    )(*results))
 
 
 def solution(mesh):

time: 81 us -> 77.9 us (0.962)
  the two profiles are of different devices: /device:TPU:1 before, /device:TPU:64 now
where the time goes in v3:
time: 77.9 us; the launch traced here: 77.7 us
  Pallas kernels  76.4 us (98%)
  between operations  1.29 us (2%)
    pallas_call x1, Pallas kernels, on_device(): pl.pallas_call(functools.partial(kernel, n, row_blocks, col_blocks, cuts)...  74.6 us
    pallas_call x1, Pallas kernels, on_device(): pl.pallas_call(store, out_shape=tuple((jax.ShapeDtypeStruct(r.shape, r.dt...  1.85 us

profile of v3, /device:TPU:64, one launch (start us, length us, event | category | flops | bytes accessed | tf_op | source)
XLA Modules:
  0.0 77.7 jit_solution(17962987111549474827)
XLA Ops:
  1.3 74.6 %shard_map.85 = (bf16[16,896]{1,0:T(8,128)(2,1)}, bf16[16,256]{1,0:T(8,128)(2,1)}, bf16[1,1,14,128,128]{4,3,2,1,0:T(8,128)(2,1)}) custom-call(s32[1,1,14]{2,1,0:T(1,128)} %rows_ref.1, s32[1,1,14]{2,1,0:T(1,128)} %cols_ref.1, s32[1,1]{1,0:T(1,128)S(6)} %copy.9.count_hbm, bf16[16,256]{1,0:T(8,128)(2,1)} %tokens_ref.1, bf16[1,1,14,128,128]{4,3,2,1,0:T(8,128)(2,1)} %w_hbm.1, ...), custom_call_target="tpu_custom_call" | custom-call | tf_op jit(solution)/shard_map/pallas_call | solution.py:367
  75.9 1.9 %shard_map.86 = (bf16[16,896]{1,0:T(8,128)(2,1)}, bf16[16,256]{1,0:T(8,128)(2,1)}, bf16[1,1,14,128,128]{4,3,2,1,0:T(8,128)(2,1)}) custom-call(bf16[16,896]{1,0:T(8,128)(2,1)} %get-tuple-element.6.act_ref, bf16[16,256]{1,0:T(8,128)(2,1)} %get-tuple-element.7.ig_ref, bf16[1,1,14,128,128]{4,3,2,1,0:T(8,128)(2,1)} %get-tuple-element.8.wg_ref), custom_call_target="tpu_custom_call" | custom-call | tf_op jit(solution)/shard_map/pallas_call | solution.py:408

commit v4 on v3

--- a/solution.py
+++ b/solution.py
@@ -112,6 +112,18 @@
         copy = remote(mine, mine, ax + e, ax + e, at_x(turn(x_lo, e, X_LO)))
         copy.start()
         sends.append(copy)
+
+    for e in range(1, X_LO):
+        source = turn(x_lo, -e, X_LO)
+        theirs = tok.at[z, lax.rem(source, CORES), source // CORES]
+        remote(theirs, theirs, ax + e, ax + e, at_x(source)).wait_recv()
+    az = numbers(n)
+    for o in steps:
+        to = z_other(o)
+
+        @pl.when(to != z)
+        def _():
+            remote(tok.at[z], tok.at[z], az + to, az + z, at_z(to)).start()
 
     for copy in local[1:]:
         copy.wait()
@@ -133,18 +145,6 @@
         dense_t[c * block:(c + 1) * block, r * block:(r + 1) * block] = jnp.transpose(
             w_ref[slot].astype(F32) * live
         ).astype(BF16)
-
-    for e in range(1, X_LO):
-        source = turn(x_lo, -e, X_LO)
-        theirs = tok.at[z, lax.rem(source, CORES), source // CORES]
-        remote(theirs, theirs, ax + e, ax + e, at_x(source)).wait_recv()
-    az = numbers(n)
-    for o in steps:
-        to = z_other(o)
-
-        @pl.when(to != z)
-        def _():
-            remote(tok.at[z], tok.at[z], az + to, az + z, at_z(to)).start()
 
     b1 = [numbers(n) for _ in cuts]
     b2 = [numbers(n) for _ in cuts]

time: 77.9 us -> 77.9 us (level)
  no operation moved by 1% of the time
where the time goes in v4:
time: 77.9 us; the launch traced here: 77.7 us
  Pallas kernels  76.4 us (98%)
  between operations  1.29 us (2%)
    pallas_call x1, Pallas kernels, on_device(): pl.pallas_call(functools.partial(kernel, n, row_blocks, col_blocks, cuts)...  74.5 us
    pallas_call x1, Pallas kernels, on_device(): pl.pallas_call(store, out_shape=tuple((jax.ShapeDtypeStruct(r.shape, r.dt...  1.85 us

profile of v4, /device:TPU:64, one launch (start us, length us, event | category | flops | bytes accessed | tf_op | source)
XLA Modules:
  0.0 77.7 jit_solution(5494312363996805207)
XLA Ops:
  1.3 74.5 %shard_map.85 = (bf16[16,896]{1,0:T(8,128)(2,1)}, bf16[16,256]{1,0:T(8,128)(2,1)}, bf16[1,1,14,128,128]{4,3,2,1,0:T(8,128)(2,1)}) custom-call(s32[1,1,14]{2,1,0:T(1,128)} %rows_ref.1, s32[1,1,14]{2,1,0:T(1,128)} %cols_ref.1, s32[1,1]{1,0:T(1,128)S(6)} %copy.9.count_hbm, bf16[16,256]{1,0:T(8,128)(2,1)} %tokens_ref.1, bf16[1,1,14,128,128]{4,3,2,1,0:T(8,128)(2,1)} %w_hbm.1, ...), custom_call_target="tpu_custom_call" | custom-call | tf_op jit(solution)/shard_map/pallas_call | solution.py:367
  75.8 1.9 %shard_map.86 = (bf16[16,896]{1,0:T(8,128)(2,1)}, bf16[16,256]{1,0:T(8,128)(2,1)}, bf16[1,1,14,128,128]{4,3,2,1,0:T(8,128)(2,1)}) custom-call(bf16[16,896]{1,0:T(8,128)(2,1)} %get-tuple-element.6.act_ref, bf16[16,256]{1,0:T(8,128)(2,1)} %get-tuple-element.7.ig_ref, bf16[1,1,14,128,128]{4,3,2,1,0:T(8,128)(2,1)} %get-tuple-element.8.wg_ref), custom_call_target="tpu_custom_call" | custom-call | tf_op jit(solution)/shard_map/pallas_call | solution.py:408
